TPU v7x, 32 devices: a whole 2x2x4 slice. The times are simulated.
32 devices in a mesh: cube: 8 (over z, y), blk: 4 (over x, core).
Axes of the slice: x: 2, y: 2, z: 4, core: 2. Of those that a mesh axis runs over, the one named last changes fastest.
Arguments:
- rhs_root: bfloat16 [1, 10240, 128], P(None, 'blk'), may hold values from -6 to 6
- rhs_mid: bfloat16 [2, 10240, 128], P(None, 'blk'), may hold values from -6 to 6
- rhs_leaf: bfloat16 [4, 10240, 128], P(None, 'blk'), may hold values from -6 to 6
- pivot_root: bfloat16 [2, 10240, 10240], P(None, 'cube', 'blk'), may hold values from -0.0625 to 0.0625
- pivot_mid: bfloat16 [2, 20480, 10240], P(None, 'cube', 'blk'), may hold values from -0.0625 to 0.0625
- pivot_leaf: bfloat16 [2, 40960, 10240], P(None, 'cube', 'blk'), may hold values from -0.0625 to 0.0625
- coupling_mid: bfloat16 [2, 2560, 10240], P(None, 'cube', 'blk'), may hold values from -0.0625 to 0.0625
- coupling_leaf: bfloat16 [2, 5120, 10240], P(None, 'cube', 'blk'), may hold values from -0.0625 to 0.0625
- front_blocks: int32 [7], replicated, may hold values from 40 to 80, as said below
- child_map: int32 [6, 10], replicated, may hold values from 0 to 79
Outputs:
- solution_root: bfloat16 [4, 2560, 128], P('blk', 'cube')
- solution_mid: bfloat16 [4, 5120, 128], P('blk', 'cube')
- solution_leaf: bfloat16 [4, 10240, 128], P('blk', 'cube')
Inputs may be any that keep to these rules, and one draw needn't show every extreme that they name: `front_blocks`: entry 0 is the root, entries 1 and 2 the level-1 fronts, 3 to 6 the level-2 fronts; at least one front is full in every draw. `child_map`: rows 0 and 1 belong to the level-1 fronts, row 2 + q to level-2 front q; targets may repeat within and across children.
All inputs are finite; a program needn't handle non-finite values.
Results may differ from a plain program's by a relative error of at most 0.013.
Values may be sent and summed in bfloat16 or wider, within the bound.
A program may use at most 192 MiB of HBM per device.

v0:
```python
import jax
import jax.numpy as jnp
from jax import lax
from jax.sharding import PartitionSpec as P

SEPARATOR = 10240
BLOCK_ROWS = 128


def swapped(value, axis, distance):
    return lax.ppermute(value, axis, [(i, i ^ 1 << distance) for i in range(lax.axis_size(axis))])


def rotate_parts(vec):
    half = vec.shape[1] // 2
    return jnp.concatenate([-vec[:, half:], vec[:, :half]], axis=1)


def complex_apply(matrix, vec):
    first = jnp.dot(matrix[0], vec, preferred_element_type=jnp.float32)
    second = jnp.dot(matrix[1], rotate_parts(vec), preferred_element_type=jnp.float32)
    return first + second


def complex_apply_t(matrix, vec):
    dims = (((0,), (0,)), ((), ()))
    first = lax.dot_general(matrix[0], vec, dims, preferred_element_type=jnp.float32)
    second = lax.dot_general(matrix[1], rotate_parts(vec), dims, preferred_element_type=jnp.float32)
    return first + second


def bit_set(cube_at, bit):
    return cube_at >> bit & 1 == 1


def gather_bits(piece, count, cube_at):
    for bit in range(count):
        other = swapped(piece, "cube", bit)
        upper = bit_set(cube_at, bit)
        piece = jnp.where(
            upper, jnp.concatenate([other, piece], 0), jnp.concatenate([piece, other], 0)
        )
    return piece


def swap_sum(value, bit):
    return swapped(value.astype(jnp.bfloat16), "cube", bit).astype(value.dtype)


def halve_bits(total, count, cube_at):
    for bit in reversed(range(count)):
        rows = total.shape[0] // 2
        lower = total[:rows]
        higher = total[rows:]
        upper = bit_set(cube_at, bit)
        sent = jnp.where(upper, lower, higher)
        kept = jnp.where(upper, higher, lower)
        total = kept + swap_sum(sent, bit)
    return total


def blk_total(value):
    return lax.psum(value, "blk")


def row_mask(start, count, limit):
    rows = start + jnp.arange(count, dtype=jnp.int32)
    return (rows < limit).astype(jnp.float32)[:, None]


def extend_add(gathered, targets, first_block, slice_blocks):
    blocks = gathered.reshape(targets.shape[0], BLOCK_ROWS, gathered.shape[1])
    slots = jnp.arange(slice_blocks, dtype=jnp.int32)
    placing = (targets[None, :] - first_block == slots[:, None]).astype(jnp.bfloat16)
    summed = jnp.einsum("ti,ird->trd", placing, blocks, preferred_element_type=jnp.float32)
    return summed.reshape(slice_blocks * BLOCK_ROWS, gathered.shape[1])


def pick_rows(parent_slice, targets, rows, first_row):
    block_of = rows // BLOCK_ROWS
    table = (block_of[:, None] == jnp.arange(targets.shape[0], dtype=jnp.int32)[None, :]).astype(
        jnp.int32
    )
    target_block = jnp.sum(table * targets[None, :], axis=1)
    where_row = target_block * BLOCK_ROWS + rows % BLOCK_ROWS - first_row
    inside = (where_row >= 0) & (where_row < parent_slice.shape[0])
    values = parent_slice[jnp.clip(where_row, 0, parent_slice.shape[0] - 1)].astype(jnp.float32)
    return jnp.where(inside[:, None], values, 0.0)


def forward_front(pivot, coupling, gathered, column_mask, solved_mask):
    masked = (column_mask * gathered).astype(jnp.bfloat16)
    own_rows = pivot.shape[1]
    if coupling is None:
        sums = blk_total(complex_apply(pivot, masked))
        return ((solved_mask * sums).astype(jnp.bfloat16), None)
    both = jnp.concatenate([complex_apply(pivot, masked), complex_apply(coupling, masked)], 0)
    sums = blk_total(both)
    solved = (solved_mask * sums[:own_rows]).astype(jnp.bfloat16)
    return (solved, sums[own_rows:].astype(jnp.bfloat16))


def per_device(
    rhs_root,
    rhs_mid,
    rhs_leaf,
    pivot_root,
    pivot_mid,
    pivot_leaf,
    coupling_mid,
    coupling_leaf,
    front_blocks,
    child_map,
):
    cube_n = lax.axis_size("cube")
    blk_n = lax.axis_size("blk")
    cube_at = lax.axis_index("cube")
    blk_at = lax.axis_index("blk")
    slice_rows = SEPARATOR // blk_n
    slice_blocks = slice_rows // BLOCK_ROWS
    first_row = blk_at * slice_rows
    first_block = blk_at * slice_blocks
    group_mid = cube_n // 2
    group_leaf = cube_n // 4
    bits_root = cube_n.bit_length() - 1
    bits_mid = bits_root - 1
    bits_leaf = bits_root - 2
    front_mid = cube_at // group_mid
    place_mid = cube_at % group_mid
    front_leaf = cube_at // group_leaf
    place_leaf = cube_at % group_leaf
    size_root = front_blocks[0] * BLOCK_ROWS
    size_mid = front_blocks[1 + front_mid] * BLOCK_ROWS
    size_leaf = front_blocks[3 + front_leaf] * BLOCK_ROWS
    column_leaf = row_mask(first_row, slice_rows, size_leaf)
    column_mid = row_mask(first_row, slice_rows, size_mid)
    column_root = row_mask(first_row, slice_rows, size_root)
    own_leaf = pivot_leaf.shape[1]
    gathered = lax.dynamic_index_in_dim(rhs_leaf, front_leaf, 0, keepdims=False).astype(jnp.float32)
    solved_leaf, update_leaf = forward_front(
        pivot_leaf,
        coupling_leaf,
        gathered,
        column_leaf,
        row_mask(place_leaf * own_leaf, own_leaf, size_leaf),
    )
    own_mid = pivot_mid.shape[1]
    arrived = gather_bits(update_leaf, bits_mid, cube_at)
    targets = lax.dynamic_slice_in_dim(child_map, 2 + 2 * front_mid, 2, 0).reshape(-1)
    gathered = lax.dynamic_index_in_dim(rhs_mid, front_mid, 0, keepdims=False).astype(jnp.float32)
    gathered = gathered - extend_add(arrived, targets, first_block, slice_blocks)
    solved_mid, update_mid = forward_front(
        pivot_mid,
        coupling_mid,
        gathered,
        column_mid,
        row_mask(place_mid * own_mid, own_mid, size_mid),
    )
    own_root = pivot_root.shape[1]
    arrived = gather_bits(update_mid, bits_root, cube_at)
    targets = child_map[0:2].reshape(-1)
    gathered = rhs_root[0].astype(jnp.float32) - extend_add(
        arrived, targets, first_block, slice_blocks
    )
    solved_root, unused = forward_front(
        pivot_root, None, gathered, column_root, row_mask(cube_at * own_root, own_root, size_root)
    )
    total = lax.psum(complex_apply_t(pivot_root, solved_root), "cube")
    full_root = (column_root * total).astype(jnp.bfloat16)
    piece_root = slice_rows // cube_n
    answer_root = lax.dynamic_slice_in_dim(full_root, cube_at * piece_root, piece_root, 0)
    update_rows_mid = coupling_mid.shape[1]
    rows = place_mid * update_rows_mid + jnp.arange(update_rows_mid, dtype=jnp.int32)
    targets = lax.dynamic_slice_in_dim(child_map, front_mid, 1, 0).reshape(-1)
    pulled = blk_total(pick_rows(full_root, targets, rows, first_row)).astype(jnp.bfloat16)
    term = complex_apply_t(pivot_mid, solved_mid) - complex_apply_t(coupling_mid, pulled)
    piece_mid = slice_rows // group_mid
    share = halve_bits(term, bits_mid, cube_at)
    answer_mid = (row_mask(first_row + place_mid * piece_mid, piece_mid, size_mid) * share).astype(
        jnp.bfloat16
    )
    full_mid = gather_bits(answer_mid, bits_mid, cube_at)
    update_rows_leaf = coupling_leaf.shape[1]
    rows = place_leaf * update_rows_leaf + jnp.arange(update_rows_leaf, dtype=jnp.int32)
    targets = lax.dynamic_slice_in_dim(child_map, 2 + front_leaf, 1, 0).reshape(-1)
    pulled = blk_total(pick_rows(full_mid, targets, rows, first_row)).astype(jnp.bfloat16)
    term = complex_apply_t(pivot_leaf, solved_leaf) - complex_apply_t(coupling_leaf, pulled)
    piece_leaf = slice_rows // group_leaf
    share = halve_bits(term, bits_leaf, cube_at)
    answer_leaf = (
        row_mask(first_row + place_leaf * piece_leaf, piece_leaf, size_leaf) * share
    ).astype(jnp.bfloat16)
    return (answer_root[None], answer_mid[None], answer_leaf[None])


def solution(mesh):
    in_specs = (
        P(None, "blk", None),
        P(None, "blk", None),
        P(None, "blk", None),
        P(None, "cube", "blk"),
        P(None, "cube", "blk"),
        P(None, "cube", "blk"),
        P(None, "cube", "blk"),
        P(None, "cube", "blk"),
        P(),
        P(),
    )
    out_specs = (P("blk", "cube", None), P("blk", "cube", None), P("blk", "cube", None))
    return jax.shard_map(
        per_device, mesh=mesh, in_specs=in_specs, out_specs=out_specs, check_vma=False
    )
```

profile of v0, /device:TPU:0, one launch (start us, length us, event | category | flops | bytes accessed | tf_op | source)
XLA Modules:
  0.0 470.4 jit_solution(2196238573120029285)
XLA Ops:
  11.7 3.4 fusion.65
  18.0 15.5 %fusion.2 = f32[128,5120]{1,0:T(8,128)} fusion(bf16[2,5120,2560]{2,1,0:T(8,128)(2,1)} %param.15, bf16[2560,64]{1,0:T(8,128)(2,1)S(1)} %get-tuple-element.24, bf16[2560,64]{1,0:T(8,128)(2,1)S(1)} %get-tuple-element.23), kind=kOutput, calls=%fused_computation.4 | convolution fusion | flops 3356753920 | bytes 29491200 | tf_op jit(solution)/shard_map/dot_general | solution.py:21
  33.6 15.2 %fusion.35 = f32[5120,128]{0,1:T(8,128)S(1)} fusion(f32[128,5120]{1,0:T(8,128)} %fusion.2, bf16[2,5120,2560]{2,1,0:T(8,128)(2,1)} %param.15, f32[2560]{0:T(1024)S(1)} %get-tuple-element.43, bf16[4,2560,128]{2,1,0:T(8,128)(2,1)} %param.12, s32[]{:T(128)S(6)} %select_n.217), kind=kOutput, calls=%fused_computation.35 | convolution fusion | flops 3357081600 | bytes 32122884 | tf_op jit(solution)/shard_map/dot_general | solution.py:20
  51.9 66.8 %all-reduce.7.cloned.1.call-done = f32[5760,128]{0,1:T(8,128)} async-done(((f32[5760,128]{0,1:T(8,128)}), f32[5760,128]{0,1:T(8,128)}) %all-reduce.7.cloned.1.call-update) | async-done | bytes 2949136 | tf_op jit(solution)/shard_map/psum | solution.py:63
  127.2 6.7 %collective-permute-done.1 = bf16[1280,128]{0,1:T(8,128)(2,1)S(1)} collective-permute-done((bf16[1280,128]{0,1:T(8,128)(2,1)S(1)}, bf16[1280,128]{0,1:T(8,128)(2,1)S(1)}, u32[]{:S(2)}, u32[]{:S(2)}) %collective-permute-start.1) | collective-permute-done | bytes 327712 | tf_op jit(solution)/shard_map/ppermute | solution.py:11
  139.8 7.9 %fusion.14 = f32[128,2560]{1,0:T(8,128)S(1)} fusion(bf16[2,2560,2560]{2,1,0:T(8,128)(2,1)} %param.14, bf16[2560,64]{1,0:T(8,128)(2,1)S(1)} %get-tuple-element.22, bf16[2560,64]{1,0:T(8,128)(2,1)S(1)} %get-tuple-element.21), kind=kOutput, calls=%fused_computation.16 | convolution fusion | flops 1679032320 | bytes 15073280 | tf_op jit(solution)/shard_map/dot_general | solution.py:21
  147.7 7.4 %fusion.58 = f32[2560,128]{0,1:T(8,128)S(1)} fusion(f32[128,2560]{1,0:T(8,128)S(1)} %fusion.14, bf16[2560,128]{1,0:T(8,128)(2,1)S(1)} %bitcast.160, bf16[2,2560,2560]{2,1,0:T(8,128)(2,1)} %param.14), kind=kOutput, calls=%fused_computation.50 | convolution fusion | flops 1678049280 | bytes 16384000 | tf_op jit(solution)/shard_map/dot_general | solution.py:20
  159.8 39.9 %all-reduce.9.cloned.1.call-done = f32[2880,128]{0,1:T(8,128)} async-done(((f32[2880,128]{0,1:T(8,128)}), f32[2880,128]{0,1:T(8,128)}) %all-reduce.9.cloned.1.call-update) | async-done | bytes 1474576 | tf_op jit(solution)/shard_map/psum | solution.py:63
  217.1 11.0 %collective-permute-done.4 = bf16[1280,128]{0,1:T(8,128)(2,1)S(1)} collective-permute-done((bf16[1280,128]{0,1:T(8,128)(2,1)S(1)}, bf16[1280,128]{0,1:T(8,128)(2,1)S(1)}, u32[]{:S(2)}, u32[]{:S(2)}) %collective-permute-start.4) | collective-permute-done | bytes 327712 | tf_op jit(solution)/shard_map/ppermute | solution.py:11
  231.8 5.1 %fusion.26 = f32[128,1280]{1,0:T(8,128)S(1)} fusion(bf16[2,1280,2560]{2,1,0:T(8,128)(2,1)} %param.13, bf16[2560,64]{0,1:T(8,128)(2,1)S(1)} %get-tuple-element.20, bf16[2560,64]{0,1:T(8,128)(2,1)S(1)} %get-tuple-element.19), kind=kOutput, calls=%fused_computation.28 | convolution fusion | flops 840171520 | bytes 7864320 | tf_op jit(solution)/shard_map/dot_general | solution.py:21
  236.9 6.1 %fusion.79 = f32[1280,128]{0,1:T(8,128)} fusion(f32[128,1280]{1,0:T(8,128)S(1)} %fusion.26, bf16[2560,128]{1,0:T(8,128)(2,1)S(1)} %bitcast.162, bf16[2,1280,2560]{2,1,0:T(8,128)(2,1)} %param.13), kind=kOutput, calls=%fused_computation.67 | convolution fusion | flops 839024640 | bytes 8519680 | tf_op jit(solution)/shard_map/dot_general | solution.py:20
  243.2 34.1 %all-reduce.11.cloned.1.call-done = f32[1280,128]{0,1:T(8,128)} async-done(((f32[1280,128]{0,1:T(8,128)}), f32[1280,128]{0,1:T(8,128)}) %all-reduce.11.cloned.1.call-update) | async-done | bytes 655376 | tf_op jit(solution)/shard_map/psum | solution.py:63
  278.5 3.9 fusion.24
  282.3 5.0 %fusion.49 = f32[2560,128]{0,1:T(8,128)} fusion(f32[128,2560]{1,0:T(8,128)S(1)} %fusion.24, bf16[1280,128]{0,1:T(8,128)(2,1)S(1)} %multiply_convert_fusion.2, bf16[2,1280,2560]{2,1,0:T(8,128)(2,1)} %param.13), kind=kOutput, calls=%fused_computation.47 | convolution fusion | flops 839188480 | bytes 9502720 | tf_op jit(solution)/shard_map/dot_general | solution.py:27
  287.4 5.8 %fusion.12 = f32[128,2560]{1,0:T(8,128)S(1)} fusion(bf16[2,2560,2560]{2,1,0:T(8,128)(2,1)} %param.14, bf16[2560,64]{0,1:T(8,128)(2,1)S(1)} %get-tuple-element.18, bf16[2560,64]{0,1:T(8,128)(2,1)S(1)} %get-tuple-element.17), kind=kOutput, calls=%fused_computation.14 | convolution fusion | flops 1679032320 | bytes 15073280 | tf_op jit(solution)/shard_map/dot_general | solution.py:28
  293.2 7.7 %fusion.61 = f32[128,2560]{1,0:T(8,128)} fusion(f32[128,2560]{1,0:T(8,128)S(1)} %fusion.12, bf16[2560,128]{0,1:T(8,128)(2,1)S(1)} %copy-done.4, bf16[2,2560,2560]{2,1,0:T(8,128)(2,1)} %param.14), kind=kOutput, calls=%fused_computation.51 | convolution fusion | flops 1678049280 | bytes 16384000 | tf_op jit(solution)/shard_map/dot_general | solution.py:27
  300.8 70.3 %all-reduce.13.cloned.1.call-done = f32[2560,128]{0,1:T(8,128)} async-done(((f32[2560,128]{0,1:T(8,128)}), f32[2560,128]{0,1:T(8,128)}) %all-reduce.13.cloned.1.call-update) | async-done | bytes 1310736 | tf_op jit(solution)/shard_map/psum | solution.py:168
  378.1 13.4 %all-reduce.14 = bf16[320,128]{1,0:T(8,128)(2,1)S(1)} all-reduce(f32[320,128]{1,0:T(8,128)S(1)} %convert_select_fusion.1), channel_id=1, replica_groups=mesh['cube'=8,'blk'=4] {'blk'}, use_global_device_ids=true, to_apply=%region_5.6 | all-reduce | flops 40960 | bytes 245760 | tf_op jit(solution)/shard_map/psum | solution.py:63
  395.0 7.4 %collective-permute-done.5 = bf16[1280,128]{0,1:T(8,128)(2,1)S(1)} collective-permute-done((bf16[1280,128]{0,1:T(8,128)(2,1)S(1)}, bf16[1280,128]{0,1:T(8,128)(2,1)S(1)}, u32[]{:S(2)}, u32[]{:S(2)}) %collective-permute-start.5) | collective-permute-done | bytes 327712 | tf_op jit(solution)/shard_map/ppermute | solution.py:11
  404.2 4.0 collective-permute-done.6
  409.7 10.3 %fusion = f32[128,2560]{1,0:T(8,128)S(1)} fusion(bf16[2,5120,2560]{2,1,0:T(8,128)(2,1)} %param.15, bf16[5120,64]{0,1:T(8,128)(2,1)S(1)} %get-tuple-element.16, bf16[5120,64]{0,1:T(8,128)(2,1)S(1)} %get-tuple-element.15), kind=kOutput, calls=%fused_computation.2 | convolution fusion | flops 3358064640 | bytes 28835840 | tf_op jit(solution)/shard_map/dot_general | solution.py:28
  421.5 10.5 %fusion.52 = f32[128,2560]{1,0:T(8,128)S(1)} fusion(f32[128,2560]{1,0:T(8,128)S(1)} %fusion, bf16[5120,128]{0,1:T(8,128)(2,1)S(1)} %fusion.75, bf16[2,5120,2560]{2,1,0:T(8,128)(2,1)} %param.15), kind=kOutput, calls=%fused_computation.48 | convolution fusion | flops 3355770880 | bytes 30146560 | tf_op jit(solution)/shard_map/dot_general | solution.py:27
  434.8 14.0 %all-reduce.15 = bf16[640,128]{1,0:T(8,128)(2,1)S(1)} all-reduce(f32[640,128]{1,0:T(8,128)S(1)} %convert_select_fusion), channel_id=1, replica_groups=mesh['cube'=8,'blk'=4] {'blk'}, use_global_device_ids=true, to_apply=%region_7.8 | all-reduce | flops 81920 | bytes 491520 | tf_op jit(solution)/shard_map/psum | solution.py:63
  457.5 4.9 %collective-permute-done.9 = bf16[1280,128]{0,1:T(8,128)(2,1)S(1)} collective-permute-done((bf16[1280,128]{0,1:T(8,128)(2,1)S(1)}, bf16[1280,128]{0,1:T(8,128)(2,1)S(1)}, u32[]{:S(2)}, u32[]{:S(2)}) %collective-permute-start.9) | collective-permute-done | bytes 327712 | tf_op jit(solution)/shard_map/ppermute | solution.py:11
  (151 shorter events, 77.1 us)
Async XLA Ops:
  7.2 111.5 %all-reduce.7.cloned.1.call-start = ((), (), s32[]{:S(2)}) async-start(), calls=%async_computation | async-start | bytes 5898240 | tf_op jit(solution)/shard_map/psum | solution.py:63
  50.5 76.5 %copy-start.6 = (bf16[2,2560,128]{2,1,0:T(8,128)(2,1)S(1)}, bf16[2,2560,128]{2,1,0:T(8,128)(2,1)}, u32[]{:S(2)}) copy-start(bf16[2,2560,128]{2,1,0:T(8,128)(2,1)} %param.11) | copy-start | bytes 3932164
  50.6 149.2 %all-reduce.9.cloned.1.call-start = ((), (), s32[]{:S(2)}) async-start(), calls=%async_computation.1 | async-start | bytes 3014656 | tf_op jit(solution)/shard_map/psum | solution.py:63
  119.7 5.7 %collective-permute-start = (bf16[640,128]{0,1:T(8,128)(2,1)S(1)}, bf16[640,128]{0,1:T(8,128)(2,1)S(1)}, u32[]{:S(2)}, u32[]{:S(2)}) collective-permute-start(bf16[640,128]{0,1:T(8,128)(2,1)S(1)} %slice.339), channel_id=1, source_target_pairs={{0,4},{4,0},{8,12},{12,8},{16,20},{20,16},{24,28},{28,24},{1,5},{5... | collective-permute-start | bytes 491528 | tf_op jit(solution)/shard_map/ppermute | solution.py:11
  125.5 8.4 %collective-permute-start.1 = (bf16[1280,128]{0,1:T(8,128)(2,1)S(1)}, bf16[1280,128]{0,1:T(8,128)(2,1)S(1)}, u32[]{:S(2)}, u32[]{:S(2)}) collective-permute-start(bf16[1280,128]{0,1:T(8,128)(2,1)S(1)} %maximum_select_fusion.3), channel_id=1, source_target_pairs={{0,8},{4,12},{8,0},{12,4},{16,24},{20,28},{24,16},{28,20},{1,9},{5... | collective-permute-start | bytes 983048 | tf_op jit(solution)/shard_map/ppermute | solution.py:11
  157.2 51.8 %copy-start.9 = (bf16[1,2560,128]{2,1,0:T(8,128)(2,1)S(1)}, bf16[1,2560,128]{2,1,0:T(8,128)(2,1)}, u32[]{:S(2)}) copy-start(bf16[1,2560,128]{2,1,0:T(8,128)(2,1)} %param.10) | copy-start | bytes 1966084
  157.2 120.1 %all-reduce.11.cloned.1.call-start = ((), (), s32[]{:S(2)}) async-start(), calls=%async_computation.2 | async-start | bytes 1310720 | tf_op jit(solution)/shard_map/psum | solution.py:63
  200.7 4.7 collective-permute-start.2
  206.2 5.6 %collective-permute-start.3 = (bf16[640,128]{0,1:T(8,128)(2,1)}, bf16[640,128]{0,1:T(8,128)(2,1)}, u32[]{:S(2)}, u32[]{:S(2)}) collective-permute-start(bf16[640,128]{0,1:T(8,128)(2,1)} %maximum_select_fusion.6), channel_id=1, source_target_pairs={{0,8},{4,12},{8,0},{12,4},{16,24},{20,28},{24,16},{28,20},{1,9},{5... | collective-permute-start | bytes 491528 | tf_op jit(solution)/shard_map/ppermute | solution.py:11
  209.2 6.3 %copy-start.5 = (f32[2880,128]{0,1:T(8,128)S(1)}, f32[2880,128]{0,1:T(8,128)}, u32[]{:S(2)}) copy-start(f32[2880,128]{0,1:T(8,128)} %all-reduce.9.cloned.1.call-done) | copy-start | bytes 4423684
  213.0 15.1 %collective-permute-start.4 = (bf16[1280,128]{0,1:T(8,128)(2,1)S(1)}, bf16[1280,128]{0,1:T(8,128)(2,1)S(1)}, u32[]{:S(2)}, u32[]{:S(2)}) collective-permute-start(bf16[1280,128]{0,1:T(8,128)(2,1)S(1)} %maximum_select_fusion.4), channel_id=1, source_target_pairs={{0,16},{4,20},{8,24},{12,28},{16,0},{20,4},{24,8},{28,12},{1,17},{... | collective-permute-start | bytes 983048 | tf_op jit(solution)/shard_map/ppermute | solution.py:11
  217.1 11.5 %copy-start.18 = (s32[20]{0:T(128)S(1)}, s32[20]{0:T(128)}, u32[]{:S(2)}) copy-start(s32[20]{0:T(128)} %sub.112) | copy-start | bytes 244
  231.8 5.1 %copy-start.10 = (bf16[20,128,128]{2,1,0:T(8,128)(2,1)S(1)}, bf16[20,128,128]{2,1,0:T(8,128)(2,1)}, u32[]{:S(2)}) copy-start(bf16[20,128,128]{2,1,0:T(8,128)(2,1)} %copy.75) | copy-start | bytes 1966084
  236.9 6.2 %copy-start.4 = (bf16[2560,128]{0,1:T(8,128)(2,1)S(1)}, bf16[2560,128]{0,1:T(8,128)(2,1)}, u32[]{:S(2)}) copy-start(bf16[2560,128]{0,1:T(8,128)(2,1)} %fusion.100) | copy-start | bytes 1966084
  243.1 34.2 %copy-start.12 = (f32[1280]{0:T(1024)S(1)}, f32[1280]{0:T(1024)}, u32[]{:S(2)}) copy-start(f32[1280]{0:T(1024)} %fusion.159) | copy-start | bytes 15364
  243.1 128.1 %all-reduce.13.cloned.1.call-start = ((), (), s32[]{:S(2)}) async-start(), calls=%async_computation.3 | async-start | bytes 2621440 | tf_op jit(solution)/shard_map/psum | solution.py:168
  300.8 74.9 %copy-start.14 = (s32[1024]{0:T(1024)S(1)}, s32[1024]{0:T(1024)}, u32[]{:S(2)}) copy-start(s32[1024]{0:T(1024)} %pad_clamp_fusion.1) | copy-start | bytes 12292
  371.1 20.5 %copy-start.2 = (bf16[2,320,2560]{2,1,0:T(8,128)(2,1)S(1)}, bf16[2,320,2560]{2,1,0:T(8,128)(2,1)}, u32[]{:S(2)}) copy-start(bf16[2,320,2560]{2,1,0:T(8,128)(2,1)} %param.16) | copy-start | bytes 9830404
  373.5 4.5 copy-start.17
  393.7 8.7 %collective-permute-start.5 = (bf16[1280,128]{0,1:T(8,128)(2,1)S(1)}, bf16[1280,128]{0,1:T(8,128)(2,1)S(1)}, u32[]{:S(2)}, u32[]{:S(2)}) collective-permute-start(bf16[1280,128]{0,1:T(8,128)(2,1)S(1)} %select_convert_fusion.1), channel_id=1, source_target_pairs={{0,8},{4,12},{8,0},{12,4},{16,24},{20,28},{24,16},{28,20},{1,9},{5... | collective-permute-start | bytes 983048 | tf_op jit(solution)/shard_map/ppermute | solution.py:11
  402.5 5.6 %collective-permute-start.6 = (bf16[640,128]{0,1:T(8,128)(2,1)S(1)}, bf16[640,128]{0,1:T(8,128)(2,1)S(1)}, u32[]{:S(2)}, u32[]{:S(2)}) collective-permute-start(bf16[640,128]{0,1:T(8,128)(2,1)S(1)} %select_convert_fusion.2), channel_id=1, source_target_pairs={{0,4},{4,0},{8,12},{12,8},{16,20},{20,16},{24,28},{28,24},{1,5},{5... | collective-permute-start | bytes 491528 | tf_op jit(solution)/shard_map/ppermute | solution.py:11
  408.2 11.9 %collective-permute-start.7 = (bf16[640,128]{0,1:T(8,128)(2,1)S(1)}, bf16[640,128]{0,1:T(8,128)(2,1)S(1)}, u32[]{:S(2)}, u32[]{:S(2)}) collective-permute-start(bf16[640,128]{0,1:T(8,128)(2,1)S(1)} %multiply_convert_fusion.3), channel_id=1, source_target_pairs={{0,4},{4,0},{8,12},{12,8},{16,20},{20,16},{24,28},{28,24},{1,5},{5... | collective-permute-start | bytes 491528 | tf_op jit(solution)/shard_map/ppermute | solution.py:11
  420.2 11.8 %collective-permute-start.8 = (bf16[1280,128]{0,1:T(8,128)(2,1)S(1)}, bf16[1280,128]{0,1:T(8,128)(2,1)S(1)}, u32[]{:S(2)}, u32[]{:S(2)}) collective-permute-start(bf16[1280,128]{0,1:T(8,128)(2,1)S(1)} %maximum_select_fusion.5), channel_id=1, source_target_pairs={{0,8},{4,12},{8,0},{12,4},{16,24},{20,28},{24,16},{28,20},{1,9},{5... | collective-permute-start | bytes 983048 | tf_op jit(solution)/shard_map/ppermute | solution.py:11
  454.4 8.0 %collective-permute-start.9 = (bf16[1280,128]{0,1:T(8,128)(2,1)S(1)}, bf16[1280,128]{0,1:T(8,128)(2,1)S(1)}, u32[]{:S(2)}, u32[]{:S(2)}) collective-permute-start(bf16[1280,128]{0,1:T(8,128)(2,1)S(1)} %select_convert_fusion), channel_id=1, source_target_pairs={{0,4},{4,0},{8,12},{12,8},{16,20},{20,16},{24,28},{28,24},{1,5},{5... | collective-permute-start | bytes 983048 | tf_op jit(solution)/shard_map/ppermute | solution.py:11
  (9 other events, 16.3 us)
Sparse Core Ops, SparseCore 0:
  50.7 67.9 all-reduce.6
  157.3 42.3 all-reduce.8
  243.2 34.0 all-reduce.10
  287.5 83.6 all-reduce.12
where the time goes:
time: 478 us; the launch traced here: 470 us
  waiting for transfers between devices  253 us (53%)
  matrix products  117 us (24%)
  blocking collectives  27.4 us (6%)
  local copies, waits for them, and re-layouts  22.2 us (5%)
  other arithmetic  19.3 us (4%)
  between operations  17 us (4%)
  starting transfers between devices  14 us (3%)
    psum x3, waiting for transfers between devices, blk_total(): return lax.psum(value, 'blk')  141 us
    psum x1, waiting for transfers between devices, per_device(): total = lax.psum(complex_apply_t(pivot_root, solved_root), 'cube')  70.3 us
    ppermute x10, waiting for transfers between devices, swapped(): lax.ppermute(value, axis, [(i, i ^ 1 << distance) for i in range(lax.axis...  42.2 us
    dot_general x5, matrix products, complex_apply(): jnp.dot(matrix[1], rotate_parts(vec), preferred_element_type=jnp.float32)  32.6 us
    dot_general x5, matrix products, complex_apply(): first = jnp.dot(matrix[0], vec, preferred_element_type=jnp.float32)  32 us
    psum x2, blocking collectives, blk_total(): return lax.psum(value, 'blk')  27.4 us
    dot_general x5, matrix products, complex_apply_t(): lax.dot_general(matrix[0], vec, dims, preferred_element_type=jnp.float32)  26.3 us
    dot_general x5, matrix products, complex_apply_t(): lax.dot_general(matrix[1], rotate_parts(vec), dims, preferred_element_typ...  23.4 us
  transfers between devices with their start and end apart: 14, of which 12 were waited for; matrix products, arithmetic and copies ran while one was open for 10% of the time, Pallas kernels for 0%

commit v1 on v0

--- a/solution.py
+++ b/solution.py
@@ -1,6 +1,8 @@
 import jax
 import jax.numpy as jnp
 from jax import lax
+from jax.experimental import pallas as pl
+from jax.experimental.pallas import tpu as pltpu
 from jax.sharding import PartitionSpec as P
 
 SEPARATOR = 10240
@@ -100,7 +102,7 @@
     return (solved, sums[own_rows:].astype(jnp.bfloat16))
 
 
-def per_device(
+def per_device_plain(
     rhs_root,
     rhs_mid,
     rhs_leaf,
@@ -192,6 +194,450 @@
     ).astype(jnp.bfloat16)
     return (answer_root[None], answer_mid[None], answer_leaf[None])
 
+MESH = pl.DeviceIdType.MESH
+VMEM = pltpu.VMEM
+TILE_ROWS = 256
+SLOTS = 3
+
+
+class Links:
+    def __init__(self, cube_n, blk_n):
+        self.cube_n = cube_n
+        self.blk_n = blk_n
+        self.cube = lax.axis_index("cube")
+        self.blk = lax.axis_index("blk")
+        self.used = 0
+
+    def bind(self, send, recv):
+        self.send = send
+        self.recv = recv
+
+    def start(self, src, dst, device):
+        at = self.used
+        self.used += 1
+        copy = pltpu.make_async_remote_copy(
+            src_ref=src,
+            dst_ref=dst,
+            send_sem=self.send.at[at],
+            recv_sem=self.recv.at[at],
+            device_id=device,
+            device_id_type=MESH,
+        )
+        copy.start()
+        return copy
+
+    def cube_peer(self, group, step):
+        place = lax.rem(self.cube, group)
+        other = lax.rem(place + step, group)
+        return other, (self.cube - place + other, self.blk)
+
+    def blk_peer(self, step):
+        other = lax.rem(self.blk + step, self.blk_n)
+        return other, (self.cube, other)
+
+    def core(self):
+        return lax.rem(self.blk, 2)
+
+    def chip(self):
+        return self.blk // 2
+
+    def core_peer(self):
+        other = 1 - self.core()
+        return other, (self.cube, self.chip() * 2 + other)
+
+    def chip_peer(self):
+        other = 1 - self.chip()
+        return other, (self.cube, other * 2 + self.core())
+
+    def barrier(self, group):
+        barrier = pltpu.get_barrier_semaphore()
+        peers = [self.blk_peer(k)[1] for k in range(1, self.blk_n)]
+        peers += [self.cube_peer(group, k)[1] for k in range(1, group)]
+        for peer in peers:
+            pl.semaphore_signal(barrier, inc=1, device_id=peer, device_id_type=MESH)
+        pl.semaphore_wait(barrier, len(peers))
+
+
+def wait_all(copies):
+    for copy in copies:
+        copy.wait()
+
+
+def f32(value):
+    return value.astype(jnp.float32)
+
+
+def bf16(value):
+    return value.astype(jnp.bfloat16)
+
+
+def update_chain(links, src, out, got, own, group):
+    copies = []
+    for k in range(1, links.blk_n):
+        other, device = links.blk_peer(k)
+        copies.append(links.start(src.at[other], got.at[k - 1], device))
+    yield
+    wait_all(copies)
+    total = f32(src[links.blk])
+    for k in range(1, links.blk_n):
+        total = total + f32(got[k - 1])
+    own[...] = bf16(total)
+    place = lax.rem(links.cube, group)
+    out[place, links.blk] = own[...]
+    copies = []
+    for k in range(1, group):
+        other, device = links.cube_peer(group, k)
+        copies.append(links.start(own, out.at[place, links.blk], device))
+    yield
+    wait_all(copies)
+    mine = out.at[:, links.blk]
+    other, device = links.chip_peer()
+    copies = [links.start(mine, mine, device)]
+    other, device = links.core_peer()
+    copies.append(links.start(mine, mine, device))
+    yield
+    wait_all(copies)
+    across = out.at[:, (1 - links.chip()) * 2 + links.core()]
+    copy = links.start(across, across, device)
+    yield
+    copy.wait()
+
+
+def sum_chain(links, src, out, got_core, half, got_chip, own):
+    other, device = links.core_peer()
+    copy = links.start(src.at[:, other], got_core, device)
+    yield
+    copy.wait()
+    half[...] = bf16(f32(src[:, links.core()]) + f32(got_core[...]))
+    other, device = links.chip_peer()
+    copy = links.start(half.at[other], got_chip, device)
+    yield
+    copy.wait()
+    own[...] = bf16(f32(half[links.chip()]) + f32(got_chip[...]))
+    out[links.chip(), links.core()] = own[...]
+    place = out.at[links.chip(), links.core()]
+    copy = links.start(own, place, device)
+    other, device = links.core_peer()
+    near = links.start(own, place, device)
+    yield
+    copy.wait()
+    near.wait()
+    place = out.at[1 - links.chip(), links.core()]
+    copy = links.start(place, place, device)
+    yield
+    copy.wait()
+
+
+def scatter_chain(links, src, out, got, group):
+    copies = []
+    for k in range(1, group):
+        other, device = links.cube_peer(group, k)
+        copies.append(links.start(src.at[other], got.at[k - 1], device))
+    yield
+    wait_all(copies)
+    total = f32(src[lax.rem(links.cube, group)])
+    for k in range(1, group):
+        total = total + f32(got[k - 1])
+    out[...] = bf16(total)
+
+
+def pick_chain(links, src, out, got, mid, group, rest):
+    yield from scatter_chain(links, src, mid, got, group)
+    yield from sum_chain(links, mid, out, *rest)
+
+
+def vm(*shape):
+    return VMEM(shape, jnp.bfloat16)
+
+
+def sum_scratch(rows):
+    return [vm(2, rows, 128), vm(2, rows, 128), vm(rows, 128), vm(rows, 128)]
+
+
+def chain_plan(kind, src, group):
+    shape = src.shape
+    if kind == "update":
+        n, rows = shape[0], shape[1]
+        return (
+            (group, n, rows, 128),
+            [vm(n - 1, rows, 128), vm(rows, 128)],
+            n + group + 2,
+            lambda L, s, o, t: update_chain(L, s, o, t[0], t[1], group),
+        )
+    if kind == "sum":
+        return shape, sum_scratch(shape[2]), 5, lambda L, s, o, t: sum_chain(L, s, o, *t)
+    if kind == "scatter":
+        return (
+            shape[1:],
+            [vm(group - 1, *shape[1:])],
+            group,
+            lambda L, s, o, t: scatter_chain(L, s, o, t[0], group),
+        )
+    return (
+        shape[1:],
+        [vm(group - 1, *shape[1:]), vm(*shape[1:])] + sum_scratch(shape[3]),
+        group + 5,
+        lambda L, s, o, t: pick_chain(L, s, o, t[0], t[1], group, t[2:]),
+    )
+
+
+def exchange(chains, work, collective_id, cube_n, blk_n):
+    plans = [chain_plan(kind, array, group) for kind, array, group in chains]
+    largest = max(group for _, _, group in chains)
+    n_chains = len(chains)
+    arrays = [array for _, array, _ in chains]
+    outs = [jax.ShapeDtypeStruct(plan[0], jnp.bfloat16) for plan in plans]
+    n_copies = sum(plan[2] for plan in plans)
+    scratch = [pltpu.SemaphoreType.DMA((n_copies,)), pltpu.SemaphoreType.DMA((n_copies,))]
+    for plan in plans:
+        scratch += plan[1]
+    in_specs = [pl.BlockSpec(memory_space=VMEM)] * n_chains
+    cost = None
+    if work is not None:
+        mode, matrix, vectors, first, rows = work
+        width = matrix.shape[2]
+        steps = rows // TILE_ROWS
+        arrays += [matrix, vectors]
+        in_specs += [pl.BlockSpec(memory_space=pl.ANY), pl.BlockSpec(memory_space=VMEM)]
+        if mode == "f":
+            outs.append(jax.ShapeDtypeStruct((rows, 128), jnp.bfloat16))
+        else:
+            outs.append(jax.ShapeDtypeStruct((128, width), jnp.float32))
+        scratch += [VMEM((SLOTS, 2, TILE_ROWS, width), matrix.dtype), pltpu.SemaphoreType.DMA((SLOTS,))]
+
+    def kernel(*refs):
+        n_in = len(arrays)
+        srcs, refs = refs[:n_in], refs[n_in:]
+        dsts, refs = refs[: len(outs)], refs[len(outs) :]
+        links = Links(cube_n, blk_n)
+        links.bind(refs[0], refs[1])
+        at = 2
+        running = []
+        for i, plan in enumerate(plans):
+            count = len(plan[1])
+            running.append(plan[3](links, srcs[i], dsts[i], refs[at : at + count]))
+            at += count
+
+        if work is not None:
+            a_ref, v_ref = srcs[n_chains:]
+            y_ref = dsts[n_chains]
+            buf, sems = refs[at], refs[at + 1]
+
+            def tile(i):
+                slot = lax.rem(i, SLOTS)
+                return pltpu.make_async_copy(
+                    a_ref.at[:, pl.ds(first + i * TILE_ROWS, TILE_ROWS), :], buf.at[slot], sems.at[slot]
+                )
+
+            for i in range(min(SLOTS - 1, steps)):
+                tile(i).start()
+            if mode != "f":
+                y_ref[...] = jnp.zeros_like(y_ref)
+
+            def step(i):
+                @pl.when(i + SLOTS - 1 < steps)
+                def _():
+                    tile(i + SLOTS - 1).start()
+
+                tile(i).wait()
+                slot = lax.rem(i, SLOTS)
+                at_row = pl.ds(pl.multiple_of(i * TILE_ROWS, TILE_ROWS), TILE_ROWS)
+                if mode == "f":
+                    total = jnp.dot(buf[slot, 0], v_ref[0], preferred_element_type=jnp.float32)
+                    total += jnp.dot(buf[slot, 1], v_ref[1], preferred_element_type=jnp.float32)
+                    y_ref[at_row, :] = bf16(total)
+                else:
+                    y_ref[...] += jnp.dot(
+                        v_ref[0, i], buf[slot, 0], preferred_element_type=jnp.float32
+                    ) + jnp.dot(v_ref[1, i], buf[slot, 1], preferred_element_type=jnp.float32)
+
+        links.barrier(largest)
+
+        def advance():
+            alive = []
+            for chain in running:
+                try:
+                    next(chain)
+                    alive.append(chain)
+                except StopIteration:
+                    pass
+            running[:] = alive
+
+        if work is not None:
+            parts = 5
+            cuts = [steps * j // parts for j in range(parts + 1)]
+            for lo, hi in zip(cuts, cuts[1:]):
+                advance()
+                if hi > lo:
+                    pl.loop(lo, hi)(step)
+        while running:
+            advance()
+
+    results = pl.pallas_call(
+        kernel,
+        out_shape=outs,
+        in_specs=in_specs,
+        out_specs=[pl.BlockSpec(memory_space=VMEM)] * len(outs),
+        scratch_shapes=scratch,
+        compiler_params=pltpu.CompilerParams(
+            collective_id=collective_id, has_side_effects=True, vmem_limit_bytes=60 * 1024 * 1024
+        ),
+    )(*arrays)
+    return results
+
+
+def both_parts(vec):
+    return jnp.stack([vec, rotate_parts(vec)])
+
+
+def tiles_t(vec):
+    parts = both_parts(vec)
+    return parts.reshape(2, -1, TILE_ROWS, vec.shape[1]).transpose(0, 1, 3, 2)
+
+
+def pick_blocks(piece, targets, first_block):
+    blocks = piece.reshape(-1, BLOCK_ROWS, piece.shape[1])
+    slots = jnp.arange(blocks.shape[0], dtype=jnp.int32)
+    placing = (targets[:, None] - first_block == slots[None, :]).astype(jnp.bfloat16)
+    picked = jnp.einsum("it,trd->ird", placing, blocks, preferred_element_type=jnp.float32)
+    return bf16(picked).reshape(-1, piece.shape[1])
+
+
+def per_device_fast(
+    rhs_root,
+    rhs_mid,
+    rhs_leaf,
+    pivot_root,
+    pivot_mid,
+    pivot_leaf,
+    coupling_mid,
+    coupling_leaf,
+    front_blocks,
+    child_map,
+):
+    cube_n = lax.axis_size("cube")
+    blk_n = lax.axis_size("blk")
+    cube_at = lax.axis_index("cube")
+    blk_at = lax.axis_index("blk")
+    slice_rows = rhs_root.shape[1]
+    slice_blocks = slice_rows // BLOCK_ROWS
+    first_row = blk_at * slice_rows
+    first_block = blk_at * slice_blocks
+    group_mid = cube_n // 2
+    group_leaf = cube_n // 4
+    front_mid = cube_at // group_mid
+    place_mid = cube_at % group_mid
+    front_leaf = cube_at // group_leaf
+    place_leaf = cube_at % group_leaf
+    size_root = front_blocks[0] * BLOCK_ROWS
+    size_mid = front_blocks[1 + front_mid] * BLOCK_ROWS
+    size_leaf = front_blocks[3 + front_leaf] * BLOCK_ROWS
+    column_leaf = row_mask(first_row, slice_rows, size_leaf)
+    column_mid = row_mask(first_row, slice_rows, size_mid)
+    column_root = row_mask(first_row, slice_rows, size_root)
+    own_leaf = pivot_leaf.shape[1]
+    own_mid = pivot_mid.shape[1]
+    own_root = pivot_root.shape[1]
+    half_leaf = own_leaf // 2
+
+    def by_blk(value):
+        return value.reshape(blk_n, -1, 128)
+
+    def by_core(value):
+        return value.reshape(2, 2, -1, 128)
+
+    def run(chains, work, collective_id):
+        return exchange(chains, work, collective_id, cube_n, blk_n)
+
+    gathered = f32(lax.dynamic_index_in_dim(rhs_leaf, front_leaf, 0, keepdims=False))
+    masked_leaf = bf16(column_leaf * gathered)
+    update = bf16(complex_apply(coupling_leaf, masked_leaf))
+    vec_leaf = both_parts(masked_leaf)
+    arrived, solved_low = run(
+        [("update", by_blk(update), group_mid)], ("f", pivot_leaf, vec_leaf, 0, half_leaf), 0
+    )
+    targets = lax.dynamic_slice_in_dim(child_map, 2 + 2 * front_mid, 2, 0).reshape(-1)
+    gathered = f32(lax.dynamic_index_in_dim(rhs_mid, front_mid, 0, keepdims=False))
+    gathered = gathered - extend_add(arrived.reshape(-1, 128), targets, first_block, slice_blocks)
+    masked_mid = bf16(column_mid * gathered)
+    update = bf16(complex_apply(coupling_mid, masked_mid))
+    arrived, solved_mid = run(
+        [("update", by_blk(update), cube_n)],
+        ("f", pivot_mid, both_parts(masked_mid), 0, own_mid),
+        1,
+    )
+    targets = child_map[0:2].reshape(-1)
+    gathered = f32(rhs_root[0]) - extend_add(
+        arrived.reshape(-1, 128), targets, first_block, slice_blocks
+    )
+    masked_root = bf16(column_root * gathered)
+    solved_root = bf16(complex_apply(pivot_root, masked_root))
+    solved_root, solved_mid, solved_high = run(
+        [("sum", by_core(solved_root), 1), ("sum", by_core(solved_mid), 1)],
+        ("f", pivot_leaf, vec_leaf, half_leaf, own_leaf - half_leaf),
+        2,
+    )
+    solved_root = bf16(
+        row_mask(cube_at * own_root, own_root, size_root) * f32(solved_root.reshape(-1, 128))
+    )
+    solved_mid = bf16(
+        row_mask(place_mid * own_mid, own_mid, size_mid) * f32(solved_mid.reshape(-1, 128))
+    )
+    solved_leaf = jnp.concatenate([solved_low, solved_high], 0)
+    part_root = bf16(column_root * complex_apply_t(pivot_root, solved_root))
+    targets = child_map[0:2].reshape(-1)
+    picked = pick_blocks(part_root, targets, first_block)
+    pulled, solved_leaf, term = run(
+        [
+            ("pick", picked.reshape(cube_n, 2, 2, -1, 128), cube_n),
+            ("sum", by_core(solved_leaf), 1),
+        ],
+        ("t", pivot_mid, tiles_t(solved_mid), 0, own_mid),
+        3,
+    )
+    solved_leaf = bf16(
+        row_mask(place_leaf * own_leaf, own_leaf, size_leaf) * f32(solved_leaf.reshape(-1, 128))
+    )
+    term = term.T - complex_apply_t(coupling_mid, pulled.reshape(-1, 128))
+    part_mid = bf16(column_mid * term)
+    targets = lax.dynamic_slice_in_dim(child_map, 2 + 2 * front_mid, 2, 0).reshape(-1)
+    picked = pick_blocks(part_mid, targets, first_block)
+    pulled, answer_root, term = run(
+        [
+            ("pick", picked.reshape(group_mid, 2, 2, -1, 128), group_mid),
+            ("scatter", part_root.reshape(cube_n, -1, 128), cube_n),
+        ],
+        ("t", pivot_leaf, tiles_t(solved_leaf), 0, own_leaf),
+        4,
+    )
+    term = term.T - complex_apply_t(coupling_leaf, pulled.reshape(-1, 128))
+    part_leaf = bf16(column_leaf * term)
+    answer_leaf, answer_mid = run(
+        [
+            ("scatter", part_leaf.reshape(group_leaf, -1, 128), group_leaf),
+            ("scatter", part_mid.reshape(group_mid, -1, 128), group_mid),
+        ],
+        None,
+        5,
+    )
+    return (answer_root[None], answer_mid[None], answer_leaf[None])
+
+
+def per_device(*args):
+    cube_n = lax.axis_size("cube")
+    blk_n = lax.axis_size("blk")
+    pivot_root, pivot_mid, pivot_leaf, coupling_mid = args[3], args[4], args[5], args[6]
+    fits = (
+        blk_n == 4
+        and cube_n % 4 == 0
+        and args[0].shape[2] == 128
+        and coupling_mid.shape[1] % (16 * blk_n) == 0
+        and pivot_root.shape[1] % (16 * blk_n) == 0
+        and pivot_mid.shape[1] % TILE_ROWS == 0
+        and pivot_leaf.shape[1] % (2 * TILE_ROWS) == 0
+    )
+    return per_device_fast(*args) if fits else per_device_plain(*args)
+
 
 def solution(mesh):
     in_specs = (

time: 478 us -> 249 us (0.52)
  waiting for transfers between devices: 253 us -> 0 us
  Pallas kernels: 0 us -> 166 us
  matrix products: 117 us -> 33.5 us
  blocking collectives: 27.4 us -> 0 us
  starting transfers between devices: 14 us -> 0 us
  between operations: 17 us -> 3.49 us
    psum x4 -> x0, waiting for transfers between devices: 211 us -> none  [the longest x3 141 us: blk_total(): return lax.psum(value, 'blk')]
    pallas_call x0 -> x6, Pallas kernels: none -> 166 us  [exchange(): pl.pallas_call(kernel, out_shape=outs, in_specs=in_specs, out_specs=[pl.B...]
    ppermute x10 -> x0, waiting for transfers between devices: 42.2 us -> none  [swapped(): lax.ppermute(value, axis, [(i, i ^ 1 << distance) for i in range(lax.axis...]
    psum x2 -> x0, blocking collectives: 27.4 us -> none  [blk_total(): return lax.psum(value, 'blk')]
    dot_general x5 -> x3, matrix products: 32.6 us -> 7.33 us  [complex_apply(): jnp.dot(matrix[1], rotate_parts(vec), preferred_element_type=jnp.float32)]
    dot_general x5 -> x3, matrix products: 32 us -> 7.6 us  [complex_apply(): first = jnp.dot(matrix[0], vec, preferred_element_type=jnp.float32)]
    dot_general x5 -> x3, matrix products: 26.3 us -> 7.26 us  [complex_apply_t(): lax.dot_general(matrix[0], vec, dims, preferred_element_type=jnp.float32)]
    dot_general x5 -> x3, matrix products: 23.4 us -> 7.34 us  [complex_apply_t(): lax.dot_general(matrix[1], rotate_parts(vec), dims, preferred_element_typ...]
  transfers between devices with their start and end apart: 14 -> 0, of which waited for: 12 -> 0; matrix products, arithmetic and copies ran while one was open for 10% -> 0% of each run, Pallas kernels for 0% -> 0%
where the time goes in v1:
time: 249 us; the launch traced here: 244 us
  Pallas kernels  166 us (67%)
  matrix products  33.5 us (13%)
  local copies, waits for them, and re-layouts  21 us (8%)
  other arithmetic  20.8 us (8%)
  between operations  3.49 us (1%)
    pallas_call x6, Pallas kernels, exchange(): pl.pallas_call(kernel, out_shape=outs, in_specs=in_specs, out_specs=[pl.B...  166 us
    convert_element_type x11, other arithmetic, bf16(): return value.astype(jnp.bfloat16)  10.2 us
    unnamed x43, local copies, waits for them, and re-layouts  9.36 us
    dot_general x3, matrix products, complex_apply(): first = jnp.dot(matrix[0], vec, preferred_element_type=jnp.float32)  7.6 us
    dot_general x3, matrix products, complex_apply_t(): lax.dot_general(matrix[1], rotate_parts(vec), dims, preferred_element_typ...  7.34 us
    dot_general x3, matrix products, complex_apply(): jnp.dot(matrix[1], rotate_parts(vec), preferred_element_type=jnp.float32)  7.33 us
    dot_general x3, matrix products, complex_apply_t(): lax.dot_general(matrix[0], vec, dims, preferred_element_type=jnp.float32)  7.26 us
    convert_element_type x9, local copies, waits for them, and re-layouts, bf16(): return value.astype(jnp.bfloat16)  5.69 us

profile of v1, /device:TPU:0, one launch (start us, length us, event | category | flops | bytes accessed | tf_op | source)
XLA Modules:
  0.0 244.4 jit_solution(14976436041409046831)
XLA Ops:
  0.7 1.4 fusion.148
  2.7 1.5 fusion.70
  4.9 1.8 fusion.68
  11.1 22.0 %shard_map.121 = (bf16[4,4,160,128]{3,2,1,0:T(8,128)(2,1)}, bf16[2560,128]{1,0:T(8,128)(2,1)}) custom-call(bf16[4,160,128]{2,1,0:T(8,128)(2,1)} %bitcast.199, bf16[2,5120,2560]{2,1,0:T(8,128)(2,1)} %refs_2_.5, bf16[2,2560,128]{2,1,0:T(8,128)(2,1)} %pad_maximum_fusion.refs_2_.refs_3_), custom_call_target="tpu_custom_call" | custom-call | tf_op jit(solution)/shard_map/pallas_call | solution.py:476
  34.9 1.4 fusion.63
  42.1 22.3 %shard_map.122 = (bf16[8,4,80,128]{3,2,1,0:T(8,128)(2,1)}, bf16[2560,128]{1,0:T(8,128)(2,1)}) custom-call(bf16[4,80,128]{2,1,0:T(8,128)(2,1)} %bitcast.202, bf16[2,2560,2560]{2,1,0:T(8,128)(2,1)} %refs_2_.4, bf16[2,2560,128]{2,1,0:T(8,128)(2,1)} %pad_maximum_fusion.1.refs_2_), custom_call_target="tpu_custom_call" | custom-call | tf_op jit(solution)/shard_map/pallas_call | solution.py:476
  65.5 1.4 fusion.61
  67.8 5.4 %fusion.2 = f32[128,1280]{1,0:T(8,128)S(1)} fusion(bf16[2,1280,2560]{2,1,0:T(8,128)(2,1)} %param.13, bf16[2560,64]{1,0:T(8,128)(2,1)S(1)} %get-tuple-element.38, bf16[2560,64]{1,0:T(8,128)(2,1)S(1)} %get-tuple-element.37), kind=kOutput, calls=%fused_computation.2 | convolution fusion | flops 840171520 | bytes 7864320 | tf_op jit(solution)/shard_map/dot_general | solution.py:23
  73.3 5.2 %fusion.50 = bf16[1280,128]{0,1:T(8,128)(2,1)S(1)} fusion(f32[128,1280]{1,0:T(8,128)S(1)} %fusion.2, bf16[2560,128]{1,0:T(8,128)(2,1)S(1)} %bitcast.197, bf16[2,1280,2560]{2,1,0:T(8,128)(2,1)} %param.13), kind=kOutput, calls=%fused_computation.43 | convolution fusion | flops 839188480 | bytes 8192000 | tf_op jit(solution)/shard_map/dot_general | solution.py:22
  79.4 22.3 %shard_map.123 = (bf16[2,2,320,128]{3,2,1,0:T(8,128)(2,1)}, bf16[2,2,640,128]{3,2,1,0:T(8,128)(2,1)}, bf16[2560,128]{1,0:T(8,128)(2,1)}) custom-call(bf16[2,2,320,128]{3,2,1,0:T(8,128)(2,1)} %bitcast.191, bf16[2,2,640,128]{3,2,1,0:T(8,128)(2,1)} %bitcast.198, bf16[2,5120,2560]{2,1,0:T(8,128)(2,1)} %refs_2_.5, ...), custom_call_target="tpu_custom_call" | custom-call | tf_op jit(solution)/shard_map/pallas_call | solution.py:476
  101.8 1.5 fusion.71
  108.5 4.0 %fusion = f32[128,2560]{1,0:T(8,128)S(1)} fusion(bf16[2,1280,2560]{2,1,0:T(8,128)(2,1)} %param.13, bf16[1280,64]{1,0:T(8,128)(2,1)S(1)} %get-tuple-element.44, bf16[1280,64]{1,0:T(8,128)(2,1)S(1)} %get-tuple-element.43), kind=kOutput, calls=%fused_computation | convolution fusion | flops 839516160 | bytes 8192000 | tf_op jit(solution)/shard_map/dot_general | solution.py:30
  112.7 3.9 %fusion.27 = bf16[2560,128]{0,1:T(8,128)(2,1)S(1)} fusion(f32[128,2560]{1,0:T(8,128)S(1)} %fusion, bf16[1280,128]{1,0:T(8,128)(2,1)S(1)} %bitcast.190, bf16[2,1280,2560]{2,1,0:T(8,128)(2,1)} %param.13, f32[2560]{0:T(1024)S(1)} %get-tuple-element.61), kind=kOutput, calls=%fused_computation.23 | convolution fusion | flops 839843840 | bytes 8857600 | tf_op jit(solution)/shard_map/dot_general | solution.py:29
  118.6 36.5 %shard_map.124 = (bf16[2,2,80,128]{3,2,1,0:T(8,128)(2,1)}, bf16[2,2,1280,128]{3,2,1,0:T(8,128)(2,1)}, f32[128,2560]{1,0:T(8,128)}) custom-call(bf16[8,2,2,80,128]{4,3,2,1,0:T(8,128)(2,1)} %bitcast.187, bf16[2,2,1280,128]{3,2,1,0:T(8,128)(2,1)} %bitcast.179, bf16[2,2560,2560]{2,1,0:T(8,128)(2,1)} %refs_2_.4, ...), custom_call_target="tpu_custom_call" | custom-call | tf_op jit(solution)/shard_map/pallas_call | solution.py:476
  155.1 3.3 %fusion.43 = bf16[5120,128]{1,0:T(8,128)(2,1)S(1)} fusion(f32[5120]{0:T(1024)S(1)} %fusion.116, bf16[2,2,1280,128]{3,2,1,0:T(8,128)(2,1)} %get-tuple-element.27), kind=kLoop, calls=%fused_computation.39 | loop fusion | flops 1966080 | bytes 2641920 | tf_op jit(solution)/shard_map/convert_element_type | solution.py:271
  159.7 1.5 copy.74
  161.1 1.8 copy.73
  164.3 1.7 maximum_bitcast_fusion.refs_3_
  171.1 41.6 %shard_map.125 = (bf16[2,2,160,128]{3,2,1,0:T(8,128)(2,1)}, bf16[320,128]{1,0:T(8,128)(2,1)}, f32[128,2560]{1,0:T(8,128)}) custom-call(bf16[4,2,2,160,128]{4,3,2,1,0:T(8,128)(2,1)} %bitcast.182, bf16[8,320,128]{2,1,0:T(8,128)(2,1)} %bitcast.175, bf16[2,5120,2560]{2,1,0:T(8,128)(2,1)} %refs_2_.5, bf16[2,20,128,256]{3,2,1,0:T(8,128)(2,1)} %maximum_bitcast_fusion.refs_3_), custom_call_target="tpu_custom_call" | custom-call | tf_op jit(solution)/shard_map/pallas_call | solution.py:476
  212.7 2.8 %fusion.35 = f32[128,2560]{1,0:T(8,128)S(1)} fusion(bf16[640,128]{1,0:T(8,128)(2,1)} %bitcast.188, bf16[2,640,2560]{2,1,0:T(8,128)(2,1)} %param.17), kind=kOutput, calls=%fused_computation.29 | convolution fusion | flops 419430400 | bytes 4751360 | tf_op jit(solution)/shard_map/dot_general | solution.py:29
  215.7 2.7 %fusion.31 = bf16[2560,128]{0,1:T(8,128)(2,1)S(1)} fusion(f32[128,2560]{1,0:T(8,128)S(1)} %copy-done.12, f32[128,2560]{1,0:T(8,128)S(1)} %fusion.35, bf16[2,640,2560]{2,1,0:T(8,128)(2,1)} %param.17, f32[2560]{0:T(1024)S(1)} %fusion.129, bf16[640,64]{1,0:T(8,128)(2,1)S(1)} %get-tuple-element.46, bf16[640,64]{1,0:T(8,128)(2,1)S(1)} %get-tuple-element.45), kind=kOutput, calls=%fused_computation.25 | convolution fusion | flops 421068800 | bytes 6727680 | tf_op jit(solution)/shard_map/dot_general | solution.py:30
  219.5 20.8 %shard_map.126 = (bf16[1280,128]{1,0:T(8,128)(2,1)}, bf16[640,128]{1,0:T(8,128)(2,1)}) custom-call(bf16[2,1280,128]{2,1,0:T(8,128)(2,1)} %bitcast.185, bf16[4,640,128]{2,1,0:T(8,128)(2,1)} %bitcast.177), custom_call_target="tpu_custom_call" | custom-call | tf_op jit(solution)/shard_map/pallas_call | solution.py:476
  240.9 1.6 copy.103
  242.5 1.7 copy.104
  (101 shorter events, 31.0 us)
Async XLA Ops:
  4.2 3.6 %copy-start.2 = (bf16[2,640,2560]{2,1,0:T(8,128)(2,1)S(1)}, bf16[2,640,2560]{2,1,0:T(8,128)(2,1)}, u32[]{:S(2)}) copy-start(bf16[2,640,2560]{2,1,0:T(8,128)(2,1)} %param.17) | copy-start | bytes 19660804
  11.1 22.1 %copy-start.6 = (bf16[2,2560,128]{2,1,0:T(8,128)(2,1)S(1)}, bf16[2,2560,128]{2,1,0:T(8,128)(2,1)}, u32[]{:S(2)}) copy-start(bf16[2,2560,128]{2,1,0:T(8,128)(2,1)} %param.11) | copy-start | bytes 3932164
  33.2 1.6 copy-start.19
  33.2 1.7 copy-start.13
  37.7 2.4 copy-start.4
  42.1 22.5 %copy-start.7 = (bf16[1,2560,128]{2,1,0:T(8,128)(2,1)S(1)}, bf16[1,2560,128]{2,1,0:T(8,128)(2,1)}, u32[]{:S(2)}) copy-start(bf16[1,2560,128]{2,1,0:T(8,128)(2,1)} %param.10) | copy-start | bytes 1966084
  64.4 1.1 copy-start.14
  103.6 1.1 copy-start.8
  105.1 1.2 copy-start.16
  105.1 1.8 copy-start.17
  106.9 1.2 copy-start.10
  117.0 1.6 copy-start
  162.9 1.3 copy-start.3
  164.3 2.9 %copy-start.5 = (bf16[2,320,2560]{2,1,0:T(8,128)(2,1)S(1)}, bf16[2,320,2560]{2,1,0:T(8,128)(2,1)}, u32[]{:S(2)}) copy-start(bf16[2,320,2560]{2,1,0:T(8,128)(2,1)} %param.16) | copy-start | bytes 9830404
  164.3 2.9 %copy-start.15 = (bf16[2,2,80,128]{3,2,1,0:T(8,128)(2,1)S(1)}, bf16[2,2,80,128]{3,2,1,0:T(8,128)(2,1)}, u32[]{:S(2)}) copy-start(bf16[2,2,80,128]{3,2,1,0:T(8,128)(2,1)} %get-tuple-element.26) | copy-start | bytes 245764
  167.1 1.3 copy-start.11
  169.4 1.7 copy-start.1
  212.7 2.8 %copy-start.9 = (bf16[2,2,160,128]{3,2,1,0:T(8,128)(2,1)S(1)}, bf16[2,2,160,128]{3,2,1,0:T(8,128)(2,1)}, u32[]{:S(2)}) copy-start(bf16[2,2,160,128]{3,2,1,0:T(8,128)(2,1)} %get-tuple-element.30) | copy-start | bytes 491524
  212.7 3.0 %copy-start.12 = (f32[128,2560]{1,0:T(8,128)S(1)}, f32[128,2560]{1,0:T(8,128)}, u32[]{:S(2)}) copy-start(f32[128,2560]{1,0:T(8,128)} %get-tuple-element.29) | copy-start | bytes 3932164
  218.4 21.9 %copy-start.18 = (bf16[320,128]{1,0:T(8,128)(2,1)S(1)}, bf16[320,128]{1,0:T(8,128)(2,1)}, u32[]{:S(2)}) copy-start(bf16[320,128]{1,0:T(8,128)(2,1)} %get-tuple-element.28) | copy-start | bytes 245764

commit v2 on v1

--- a/solution.py
+++ b/solution.py
@@ -328,12 +328,15 @@
     copy.wait()
 
 
-def scatter_chain(links, src, out, got, group):
+def scatter_chain(links, src, out, got, group, before=0, beside=1):
+    for _ in range(before):
+        yield
     copies = []
     for k in range(1, group):
         other, device = links.cube_peer(group, k)
         copies.append(links.start(src.at[other], got.at[k - 1], device))
-    yield
+    for _ in range(beside):
+        yield
     wait_all(copies)
     total = f32(src[lax.rem(links.cube, group)])
     for k in range(1, group):
@@ -371,7 +374,7 @@
             shape[1:],
             [vm(group - 1, *shape[1:])],
             group,
-            lambda L, s, o, t: scatter_chain(L, s, o, t[0], group),
+            lambda L, s, o, t: scatter_chain(L, s, o, t[0], group, 1, 4),
         )
     return (
         shape[1:],
@@ -447,9 +450,9 @@
                     total += jnp.dot(buf[slot, 1], v_ref[1], preferred_element_type=jnp.float32)
                     y_ref[at_row, :] = bf16(total)
                 else:
-                    y_ref[...] += jnp.dot(
-                        v_ref[0, i], buf[slot, 0], preferred_element_type=jnp.float32
-                    ) + jnp.dot(v_ref[1, i], buf[slot, 1], preferred_element_type=jnp.float32)
+                    both = buf[slot].reshape(2 * TILE_ROWS, width)
+                    vec = jnp.concatenate([v_ref[0, i], v_ref[1, i]], axis=1)
+                    y_ref[...] += jnp.dot(vec, both, preferred_element_type=jnp.float32)
 
         links.barrier(largest)
 
@@ -561,8 +564,8 @@
     gathered = gathered - extend_add(arrived.reshape(-1, 128), targets, first_block, slice_blocks)
     masked_mid = bf16(column_mid * gathered)
     update = bf16(complex_apply(coupling_mid, masked_mid))
-    arrived, solved_mid = run(
-        [("update", by_blk(update), cube_n)],
+    arrived, solved_low, solved_mid = run(
+        [("update", by_blk(update), cube_n), ("sum", by_core(solved_low), 1)],
         ("f", pivot_mid, both_parts(masked_mid), 0, own_mid),
         1,
     )
@@ -583,42 +586,40 @@
     solved_mid = bf16(
         row_mask(place_mid * own_mid, own_mid, size_mid) * f32(solved_mid.reshape(-1, 128))
     )
-    solved_leaf = jnp.concatenate([solved_low, solved_high], 0)
     part_root = bf16(column_root * complex_apply_t(pivot_root, solved_root))
     targets = child_map[0:2].reshape(-1)
     picked = pick_blocks(part_root, targets, first_block)
-    pulled, solved_leaf, term = run(
+    pulled, solved_high, term = run(
         [
             ("pick", picked.reshape(cube_n, 2, 2, -1, 128), cube_n),
-            ("sum", by_core(solved_leaf), 1),
+            ("sum", by_core(solved_high), 1),
         ],
         ("t", pivot_mid, tiles_t(solved_mid), 0, own_mid),
         3,
     )
-    solved_leaf = bf16(
-        row_mask(place_leaf * own_leaf, own_leaf, size_leaf) * f32(solved_leaf.reshape(-1, 128))
-    )
+    first_leaf = place_leaf * own_leaf
+    mask_low = row_mask(first_leaf, half_leaf, size_leaf)
+    mask_high = row_mask(first_leaf + half_leaf, own_leaf - half_leaf, size_leaf)
+    tiles_low = tiles_t(bf16(mask_low * f32(solved_low.reshape(-1, 128))))
+    tiles_high = tiles_t(bf16(mask_high * f32(solved_high.reshape(-1, 128))))
+    tiles_leaf = jnp.concatenate([tiles_low, tiles_high], 1)
     term = term.T - complex_apply_t(coupling_mid, pulled.reshape(-1, 128))
     part_mid = bf16(column_mid * term)
     targets = lax.dynamic_slice_in_dim(child_map, 2 + 2 * front_mid, 2, 0).reshape(-1)
     picked = pick_blocks(part_mid, targets, first_block)
-    pulled, answer_root, term = run(
+    pulled, answer_root, answer_mid, term = run(
         [
             ("pick", picked.reshape(group_mid, 2, 2, -1, 128), group_mid),
             ("scatter", part_root.reshape(cube_n, -1, 128), cube_n),
+            ("scatter", part_mid.reshape(group_mid, -1, 128), group_mid),
         ],
-        ("t", pivot_leaf, tiles_t(solved_leaf), 0, own_leaf),
+        ("t", pivot_leaf, tiles_leaf, 0, own_leaf),
         4,
     )
     term = term.T - complex_apply_t(coupling_leaf, pulled.reshape(-1, 128))
     part_leaf = bf16(column_leaf * term)
-    answer_leaf, answer_mid = run(
-        [
-            ("scatter", part_leaf.reshape(group_leaf, -1, 128), group_leaf),
-            ("scatter", part_mid.reshape(group_mid, -1, 128), group_mid),
-        ],
-        None,
-        5,
+    (answer_leaf,) = run(
+        [("scatter", part_leaf.reshape(group_leaf, -1, 128), group_leaf)], None, 5
     )
     return (answer_root[None], answer_mid[None], answer_leaf[None])
 
@@ -633,6 +634,7 @@
         and args[0].shape[2] == 128
         and coupling_mid.shape[1] % (16 * blk_n) == 0
         and pivot_root.shape[1] % (16 * blk_n) == 0
+        and pivot_leaf.shape[1] % (32 * blk_n) == 0
         and pivot_mid.shape[1] % TILE_ROWS == 0
         and pivot_leaf.shape[1] % (2 * TILE_ROWS) == 0
     )

time: 249 us -> 228 us (0.916)
  Pallas kernels: 166 us -> 151 us
  matrix products: 33.5 us -> 30.9 us
    pallas_call x6, Pallas kernels: 166 us -> 151 us  [exchange(): pl.pallas_call(kernel, out_shape=outs, in_specs=in_specs, out_specs=[pl.B...]
    dot_general x3, matrix products: 7.6 us -> 4.75 us  [complex_apply(): first = jnp.dot(matrix[0], vec, preferred_element_type=jnp.float32)]
    unnamed x43 -> x47, local copies, waits for them, and re-layouts: 9.36 us -> 7.01 us
    convert_element_type x11 -> x13, other arithmetic: 10.2 us -> 9.91 us  [bf16(): return value.astype(jnp.bfloat16)]
where the time goes in v2:
time: 228 us; the launch traced here: 224 us
  Pallas kernels  151 us (66%)
  matrix products  30.9 us (14%)
  other arithmetic  19.7 us (9%)
  local copies, waits for them, and re-layouts  18.6 us (8%)
  between operations  3.63 us (2%)
    pallas_call x6, Pallas kernels, exchange(): pl.pallas_call(kernel, out_shape=outs, in_specs=in_specs, out_specs=[pl.B...  151 us
    convert_element_type x13, other arithmetic, bf16(): return value.astype(jnp.bfloat16)  9.91 us
    dot_general x3, matrix products, complex_apply(): jnp.dot(matrix[1], rotate_parts(vec), preferred_element_type=jnp.float32)  7.62 us
    dot_general x3, matrix products, complex_apply_t(): lax.dot_general(matrix[1], rotate_parts(vec), dims, preferred_element_typ...  7.33 us
    dot_general x3, matrix products, complex_apply_t(): lax.dot_general(matrix[0], vec, dims, preferred_element_type=jnp.float32)  7.26 us
    unnamed x47, local copies, waits for them, and re-layouts  7.01 us
    convert_element_type x9, local copies, waits for them, and re-layouts, bf16(): return value.astype(jnp.bfloat16)  5.73 us
    dot_general x3, matrix products, complex_apply(): first = jnp.dot(matrix[0], vec, preferred_element_type=jnp.float32)  4.75 us

profile of v2, /device:TPU:0, one launch (start us, length us, event | category | flops | bytes accessed | tf_op | source)
XLA Modules:
  0.0 223.6 jit_solution(11765977115513405093)
XLA Ops:
  0.7 1.4 fusion.151
  2.7 1.5 fusion.69
  4.9 1.8 fusion.67
  11.2 22.0 %shard_map.121 = (bf16[4,4,160,128]{3,2,1,0:T(8,128)(2,1)}, bf16[2560,128]{1,0:T(8,128)(2,1)}) custom-call(bf16[4,160,128]{2,1,0:T(8,128)(2,1)} %bitcast.215, bf16[2,5120,2560]{2,1,0:T(8,128)(2,1)} %refs_3_.1, bf16[2,2560,128]{2,1,0:T(8,128)(2,1)} %pad_maximum_fusion.1.refs_2_.refs_3_), custom_call_target="tpu_custom_call" | custom-call | tf_op jit(solution)/shard_map/pallas_call | solution.py:479
  35.0 1.4 fusion.62
  42.2 26.0 %shard_map.122 = (bf16[8,4,80,128]{3,2,1,0:T(8,128)(2,1)}, bf16[2,2,640,128]{3,2,1,0:T(8,128)(2,1)}, bf16[2560,128]{1,0:T(8,128)(2,1)}) custom-call(bf16[4,80,128]{2,1,0:T(8,128)(2,1)} %bitcast.217, bf16[2,2,640,128]{3,2,1,0:T(8,128)(2,1)} %bitcast.210, bf16[2,2560,2560]{2,1,0:T(8,128)(2,1)} %refs_2_.5, bf16[2,2560,128]{2,1,0:T(8,128)(2,1)} %pad_maximum_fusion.2.refs_3_), custom_call_target="tpu_custom_call" | custom-call | tf_op jit(solution)/shard_map/pallas_call | solution.py:479
  68.2 1.5 fusion.71
  72.8 1.3 fusion.60
  75.1 5.7 %fusion.2 = f32[128,1280]{1,0:T(8,128)S(1)} fusion(bf16[2,1280,2560]{2,1,0:T(8,128)(2,1)} %param.13, bf16[2560,64]{1,0:T(8,128)(2,1)S(1)} %get-tuple-element.40, bf16[2560,64]{1,0:T(8,128)(2,1)S(1)} %get-tuple-element.39), kind=kOutput, calls=%fused_computation.2 | convolution fusion | flops 840171520 | bytes 7864320 | tf_op jit(solution)/shard_map/dot_general | solution.py:23
  81.0 2.3 %fusion.49 = bf16[1280,128]{0,1:T(8,128)(2,1)S(1)} fusion(f32[128,1280]{1,0:T(8,128)S(1)} %fusion.2, bf16[2560,128]{1,0:T(8,128)(2,1)S(1)} %bitcast.212, bf16[2,1280,2560]{2,1,0:T(8,128)(2,1)S(1)} %bitcast.184), kind=kOutput, calls=%fused_computation.40 | convolution fusion | flops 839188480 | bytes 8192000 | tf_op jit(solution)/shard_map/dot_general | solution.py:22
  84.2 21.9 %shard_map.123 = (bf16[2,2,320,128]{3,2,1,0:T(8,128)(2,1)}, bf16[2,2,640,128]{3,2,1,0:T(8,128)(2,1)}, bf16[2560,128]{1,0:T(8,128)(2,1)}) custom-call(bf16[2,2,320,128]{3,2,1,0:T(8,128)(2,1)} %bitcast.205, bf16[2,2,640,128]{3,2,1,0:T(8,128)(2,1)} %bitcast.214, bf16[2,5120,2560]{2,1,0:T(8,128)(2,1)} %refs_3_.1, ...), custom_call_target="tpu_custom_call" | custom-call | tf_op jit(solution)/shard_map/pallas_call | solution.py:479
  106.2 1.5 fusion.72
  108.6 1.3 copy.69
  111.8 4.0 %fusion = f32[128,2560]{1,0:T(8,128)S(1)} fusion(bf16[2,1280,2560]{2,1,0:T(8,128)(2,1)} %param.13, bf16[1280,64]{1,0:T(8,128)(2,1)S(1)} %get-tuple-element.46, bf16[1280,64]{1,0:T(8,128)(2,1)S(1)} %get-tuple-element.45), kind=kOutput, calls=%fused_computation | convolution fusion | flops 839516160 | bytes 8192000 | tf_op jit(solution)/shard_map/dot_general | solution.py:30
  116.0 3.9 %fusion.27 = bf16[2560,128]{0,1:T(8,128)(2,1)S(1)} fusion(f32[128,2560]{1,0:T(8,128)S(1)} %fusion, bf16[1280,128]{1,0:T(8,128)(2,1)S(1)} %bitcast.203, bf16[2,1280,2560]{2,1,0:T(8,128)(2,1)} %param.13, f32[2560]{0:T(1024)S(1)} %get-tuple-element.63), kind=kOutput, calls=%fused_computation.23 | convolution fusion | flops 839843840 | bytes 8857600 | tf_op jit(solution)/shard_map/dot_general | solution.py:29
  121.9 31.8 %shard_map.124 = (bf16[2,2,80,128]{3,2,1,0:T(8,128)(2,1)}, bf16[2,2,640,128]{3,2,1,0:T(8,128)(2,1)}, f32[128,2560]{1,0:T(8,128)}) custom-call(bf16[8,2,2,80,128]{4,3,2,1,0:T(8,128)(2,1)} %bitcast.200, bf16[2,2,640,128]{3,2,1,0:T(8,128)(2,1)} %bitcast.213, bf16[2,2560,2560]{2,1,0:T(8,128)(2,1)} %refs_2_.5, bf16[2,10,128,256]{3,2,1,0:T(8,128)(2,1)} %maximum_bitcast_fusion.refs_3_), custom_call_target="tpu_custom_call" | custom-call | tf_op jit(solution)/shard_map/pallas_call | solution.py:479
  153.7 1.5 fusion.70
  156.1 1.3 copy.78
  157.8 1.7 pad_maximum_fusion.refs_4_
  164.6 36.3 %shard_map.125 = (bf16[2,2,160,128]{3,2,1,0:T(8,128)(2,1)}, bf16[320,128]{1,0:T(8,128)(2,1)}, bf16[640,128]{1,0:T(8,128)(2,1)}, f32[128,2560]{1,0:T(8,128)}) custom-call(bf16[4,2,2,160,128]{4,3,2,1,0:T(8,128)(2,1)} %bitcast.191, bf16[8,320,128]{2,1,0:T(8,128)(2,1)} %bitcast.187, bf16[4,640,128]{2,1,0:T(8,128)(2,1)} %bitcast.189, ...), custom_call_target="tpu_custom_call" | custom-call | tf_op jit(solution)/shard_map/pallas_call | solution.py:479
  200.8 2.8 %fusion.35 = f32[128,2560]{1,0:T(8,128)S(1)} fusion(bf16[640,128]{1,0:T(8,128)(2,1)} %bitcast.201, bf16[2,640,2560]{2,1,0:T(8,128)(2,1)} %param.17), kind=kOutput, calls=%fused_computation.29 | convolution fusion | flops 419430400 | bytes 4751360 | tf_op jit(solution)/shard_map/dot_general | solution.py:29
  203.8 2.7 %fusion.31 = bf16[2560,128]{0,1:T(8,128)(2,1)S(1)} fusion(f32[128,2560]{1,0:T(8,128)S(1)} %copy-done.11, f32[128,2560]{1,0:T(8,128)S(1)} %fusion.35, bf16[2,640,2560]{2,1,0:T(8,128)(2,1)} %param.17, f32[2560]{0:T(1024)S(1)} %get-tuple-element.66, bf16[640,64]{1,0:T(8,128)(2,1)S(1)} %get-tuple-element.48, bf16[640,64]{1,0:T(8,128)(2,1)S(1)} %get-tuple-element.47), kind=kOutput, calls=%fused_computation.25 | convolution fusion | flops 421068800 | bytes 6727680 | tf_op jit(solution)/shard_map/dot_general | solution.py:30
  207.6 12.7 %shard_map.126 = bf16[1280,128]{1,0:T(8,128)(2,1)} custom-call(bf16[2,1280,128]{2,1,0:T(8,128)(2,1)} %bitcast.196), custom_call_target="tpu_custom_call" | custom-call | tf_op jit(solution)/shard_map/pallas_call | solution.py:479
  221.7 1.7 copy.108
  (113 shorter events, 29.9 us)
Async XLA Ops:
  4.2 3.7 %copy-start.2 = (bf16[2,640,2560]{2,1,0:T(8,128)(2,1)S(1)}, bf16[2,640,2560]{2,1,0:T(8,128)(2,1)}, u32[]{:S(2)}) copy-start(bf16[2,640,2560]{2,1,0:T(8,128)(2,1)} %param.17) | copy-start | bytes 19660804
  11.2 22.1 %copy-start.5 = (bf16[2,2560,128]{2,1,0:T(8,128)(2,1)S(1)}, bf16[2,2560,128]{2,1,0:T(8,128)(2,1)}, u32[]{:S(2)}) copy-start(bf16[2,2560,128]{2,1,0:T(8,128)(2,1)} %param.11) | copy-start | bytes 3932164
  33.2 1.6 copy-start.17
  33.2 1.7 copy-start.12
  37.7 2.4 %copy-start.3 = (bf16[2,320,2560]{2,1,0:T(8,128)(2,1)S(1)}, bf16[2,320,2560]{2,1,0:T(8,128)(2,1)}, u32[]{:S(2)}) copy-start(bf16[2,320,2560]{2,1,0:T(8,128)(2,1)} %param.16) | copy-start | bytes 9830404
  69.9 1.1 copy-start.7
  71.5 1.1 copy-start.6
  71.5 9.4 %slice-start = ((s8[13107200]{0:T(1024)(128)(4,1)}), s8[524288]{0:T(1024)(128)(4,1)S(1)}, s32[]{:S(2)}) async-start(s8[13107200]{0:T(1024)(128)(4,1)} %bitcast.183), calls=%async_computation | async-start | bytes 1048576
  71.6 1.2 copy-start.13
  72.8 8.1 %slice-start.1 = ((s8[13107200]{0:T(1024)(128)(4,1)}), s8[4194304]{0:T(1024)(128)(4,1)S(1)}, s32[]{:S(2)}) async-start(s8[13107200]{0:T(1024)(128)(4,1)} %bitcast.183), calls=%async_computation.1 | async-start | bytes 8388608
  74.4 6.5 %slice-start.2 = ((s8[13107200]{0:T(1024)(128)(4,1)}), s8[4194304]{0:T(1024)(128)(4,1)S(1)}, s32[]{:S(2)}) async-start(s8[13107200]{0:T(1024)(128)(4,1)} %bitcast.183), calls=%async_computation.2 | async-start | bytes 8388608
  75.1 5.8 %slice-start.3 = ((s8[13107200]{0:T(1024)(128)(4,1)}), s8[4194304]{0:T(1024)(128)(4,1)S(1)}, s32[]{:S(2)}) async-start(s8[13107200]{0:T(1024)(128)(4,1)} %bitcast.183), calls=%async_computation.3 | async-start | bytes 8388608
  110.1 1.3 copy-start.9
  120.3 1.7 copy-start
  157.8 2.9 %copy-start.4 = (bf16[2,320,2560]{2,1,0:T(8,128)(2,1)S(1)}, bf16[2,320,2560]{2,1,0:T(8,128)(2,1)}, u32[]{:S(2)}) copy-start(bf16[2,320,2560]{2,1,0:T(8,128)(2,1)} %param.16) | copy-start | bytes 9830404
  157.8 2.9 %copy-start.14 = (bf16[2,2,80,128]{3,2,1,0:T(8,128)(2,1)S(1)}, bf16[2,2,80,128]{3,2,1,0:T(8,128)(2,1)}, u32[]{:S(2)}) copy-start(bf16[2,2,80,128]{3,2,1,0:T(8,128)(2,1)} %get-tuple-element.26) | copy-start | bytes 245764
  160.6 1.3 copy-start.10
  162.9 1.7 copy-start.1
  200.8 2.8 %copy-start.8 = (bf16[2,2,160,128]{3,2,1,0:T(8,128)(2,1)S(1)}, bf16[2,2,160,128]{3,2,1,0:T(8,128)(2,1)}, u32[]{:S(2)}) copy-start(bf16[2,2,160,128]{3,2,1,0:T(8,128)(2,1)} %get-tuple-element.32) | copy-start | bytes 491524
  200.8 3.0 %copy-start.11 = (f32[128,2560]{1,0:T(8,128)S(1)}, f32[128,2560]{1,0:T(8,128)}, u32[]{:S(2)}) copy-start(f32[128,2560]{1,0:T(8,128)} %get-tuple-element.31) | copy-start | bytes 3932164
  206.5 13.8 %copy-start.16 = (bf16[320,128]{1,0:T(8,128)(2,1)S(1)}, bf16[320,128]{1,0:T(8,128)(2,1)}, u32[]{:S(2)}) copy-start(bf16[320,128]{1,0:T(8,128)(2,1)} %get-tuple-element.29) | copy-start | bytes 245764
  206.5 14.5 %copy-start.15 = (bf16[640,128]{1,0:T(8,128)(2,1)S(1)}, bf16[640,128]{1,0:T(8,128)(2,1)}, u32[]{:S(2)}) copy-start(bf16[640,128]{1,0:T(8,128)(2,1)} %get-tuple-element.30) | copy-start | bytes 491524
